TPU v7x, 32 devices: a whole 2x2x4 slice. The times are simulated.
32 devices in a mesh: integral: 4 (over x, core), pair: 8 (over z, y).
Axes of the slice: x: 2, y: 2, z: 4, core: 2. Of those that a mesh axis runs over, the one named last changes fastest.
Arguments:
- t2_tiles: bfloat16 [1024, 20, 1024], P('pair', None, 'integral'), may hold values from -6 to 6
- keep_tile: int32 [20], replicated, may hold values from 0 to 31, as said below
- integrals: bfloat16 [32, 1024, 4096], P('pair', None, 'integral'), may hold values from -0.078125 to 0.078125
Outputs:
- residual: bfloat16 [1024, 4096], P('pair', 'integral')
Inputs may be any that keep to these rules, and one draw needn't show every extreme that they name: `keep_tile`: 20 distinct tile numbers in no particular order; tile k lies in the integral rows of pair index k // 4; at least one pair index has all 4 of its tiles listed.
All inputs are finite; a program needn't handle non-finite values.
Results may differ from a plain program's by a relative error of at most 0.0014.
Values may be sent and summed in bfloat16 or wider, within the bound.
A program may use at most 128 MiB of HBM per device.

v0:
```python
import jax
import jax.numpy as jnp
from jax import lax
from jax.sharding import PartitionSpec as P


def on_device(t2_tiles, keep_tile, integrals):
    pair_count = lax.axis_size("pair")
    myself = lax.axis_index("pair")
    op_dev = t2_tiles.shape[0]
    kept_count = t2_tiles.shape[1]
    slot_count = integrals.shape[0]
    owners = keep_tile // slot_count
    positions = jnp.arange(kept_count, dtype=jnp.int32)
    earlier = (positions[None, :] < positions[:, None]) & (owners[None, :] == owners[:, None])
    ranking = jnp.sum(earlier.astype(jnp.int32), axis=1)
    matches = (ranking[:, None, None] == jnp.arange(slot_count, dtype=jnp.int32)[None, :, None]) & (
        owners[:, None, None] == jnp.arange(pair_count, dtype=jnp.int32)[None, None, :]
    )
    match_ints = matches.astype(jnp.int32)
    filled = jnp.sum(match_ints, axis=0)
    where_at = jnp.sum(match_ints * positions[:, None, None], axis=0)
    outgoing = jnp.take(t2_tiles, where_at.reshape(-1), axis=1)
    outgoing = outgoing.reshape(op_dev, slot_count, pair_count, t2_tiles.shape[2])
    outgoing = outgoing * filled.astype(jnp.bfloat16)[None, :, :, None]
    received = lax.all_to_all(outgoing, "pair", split_axis=2, concat_axis=0, tiled=True)
    received = received.reshape(received.shape[0], slot_count, t2_tiles.shape[2])
    my_slots = lax.dynamic_index_in_dim(where_at, myself, 1, keepdims=False)
    my_filled = lax.dynamic_index_in_dim(filled, myself, 1, keepdims=False)
    local_tile = jnp.where(my_filled > 0, jnp.take(keep_tile, my_slots) - myself * slot_count, 0)
    contract = (((1, 2), (0, 1)), ((), ()))
    chosen = jnp.take(integrals, local_tile, axis=0)
    partial_value = lax.dot_general(
        lax.all_gather(received, "integral", axis=2, tiled=True),
        chosen,
        contract,
        preferred_element_type=jnp.float32,
    )
    my_rows = lax.psum_scatter(partial_value, "pair", scatter_dimension=0, tiled=True)
    return (0.5 * my_rows).astype(jnp.bfloat16)


def solution(mesh):
    placed = (P("pair", None, "integral"), P(), P("pair", None, "integral"))
    return jax.shard_map(
        on_device, mesh=mesh, in_specs=placed, out_specs=P("pair", "integral"), check_vma=False
    )
```

profile of v0, /device:TPU:0, one launch (start us, length us, event | category | flops | bytes accessed | tf_op | source)
XLA Modules:
  0.0 239.2 jit_solution(17368932967107329152)
XLA Ops:
  6.5 0.0 copy-start
  6.5 0.0 all-gather.2.cloned.1.call-start
  6.5 0.8 and_select_fusion.1
  7.3 0.2 convert_reduce_fusion
  7.5 0.2 fusion.8
  7.7 0.1 reshape.105
  7.9 0.0 copy-done
  7.9 0.7 gather_fusion
  8.6 1.3 fusion.6
  9.9 1.2 copy.28
  11.1 55.3 %all_to_all.15 = bf16[128,4,8,256]{3,0,1,2:T(8,128)(2,1)S(1)} all-to-all(bf16[128,4,8,256]{3,0,1,2:T(8,128)(2,1)S(1)} %copy.28), channel_id=1, replica_groups=mesh['integral'=4,'pair'=8] {'pair'}, dimensions={2} | all-to-all | bytes 4194304 | tf_op jit(solution)/shard_map/all_to_all | solution.py:26
  66.4 0.0 copy-start.1
  66.4 1.5 copy.29
  67.9 0.0 all-gather.2.cloned.1.call-update
  67.9 0.0 reduce-scatter.2.cloned.1.call-start
  67.9 0.2 fusion.10
  68.1 0.0 copy-done.1
  68.1 0.6 gather_fusion.1
  68.8 0.1 copy.30
  68.9 0.2 and_reduce_fusion
  69.1 0.1 reduce.2
  69.2 6.6 %fusion.14 = (bf16[4,512,1024]{2,1,0:T(8,128)(2,1)}, bf16[4,512,1024]{2,1,0:T(8,128)(2,1)}) fusion(bf16[4,1024,1024]{2,1,0:T(8,128)(2,1)} %param.5), kind=kLoop, calls=%fused_computation.41 | loop fusion | bytes 16777216 | tf_op jit(solution)/shard_map/jit(_take)/gather | solution.py:32
  75.8 5.8 %gather_fusion.2 = bf16[4,512,1024]{2,1,0:T(8,128)(2,1)} fusion(bf16[4,512,1024]{2,1,0:T(8,128)(2,1)} %get-tuple-element.9, s32[1024]{0:T(1024)S(1)} %pad_clamp_fusion), kind=kCustom, calls=%fused_computation.2 | custom fusion | bytes 8388624 | tf_op jit(solution)/shard_map/jit(_take)/gather | solution.py:32
  81.6 5.0 %gather_fusion.3 = bf16[4,512,1024]{2,1,0:T(8,128)(2,1)} fusion(bf16[4,512,1024]{2,1,0:T(8,128)(2,1)} %get-tuple-element.10, s32[1024]{0:T(1024)S(1)} %pad_clamp_fusion), kind=kCustom, calls=%fused_computation.3 | custom fusion | bytes 8388624 | tf_op jit(solution)/shard_map/jit(_take)/gather | solution.py:32
  86.7 39.8 %all-gather.2.cloned.1.call-done = bf16[1024,4,1024]{2,0,1:T(8,128)(2,1)} async-done(((bf16[1024,4,256]{2,0,1:T(8,128)(2,1)}), bf16[1024,4,1024]{2,0,1:T(8,128)(2,1)}) %all-gather.2.cloned.1.call-update) | async-done | bytes 8388624 | tf_op jit(solution)/shard_map/all_gather | solution.py:34
  126.5 15.2 %fusion.5 = f32[1024,1024]{1,0:T(8,128)} fusion(bf16[1024,4,1024]{2,0,1:T(8,128)(2,1)} %all-gather.2.cloned.1.call-done, bf16[4,512,1024]{2,1,0:T(8,128)(2,1)} %gather_fusion.3, bf16[4,512,1024]{2,1,0:T(8,128)(2,1)} %gather_fusion.2, pred[4]{0:T(512)(128)(4,1)S(1)} %get-tuple-element.7), kind=kOutput, calls=%fused_computation.10 | convolution fusion | flops 8610906112 | bytes 20971524 | tf_op jit(solution)/shard_map/dot_general | solution.py:33
  141.7 0.0 reduce-scatter.2.cloned.1.call-update
  141.7 88.9 %reduce-scatter.2.cloned.1.call-done = f32[128,1024]{1,0:T(8,128)} async-done(((f32[1024,1024]{1,0:T(8,128)}), f32[128,1024]{1,0:T(8,128)}) %reduce-scatter.2.cloned.1.call-update) | async-done | bytes 524304 | tf_op jit(solution)/shard_map/reduce_scatter | solution.py:39
  230.6 1.8 multiply_convert_fusion
  (8 shorter events, 0.1 us)
Async XLA Ops:
  6.5 1.3 copy-start
  6.5 119.9 %all-gather.2.cloned.1.call-start = ((), (), s32[]{:S(2)}) async-start(), calls=%async_computation.2 | async-start | bytes 10485760 | tf_op jit(solution)/shard_map/all_gather | solution.py:34
  66.4 1.7 copy-start.1
  67.9 162.7 %reduce-scatter.2.cloned.1.call-start = ((), (), s32[]{:S(2)}) async-start(), calls=%async_computation.3 | async-start | bytes 4718592 | tf_op jit(solution)/shard_map/reduce_scatter | solution.py:39
Sparse Core Ops, SparseCore 0:
  68.0 58.4 all-gather.1
  141.8 88.7 reduce-scatter.1
where the time goes:
time: 239 us
  waiting for transfers between devices  129 us (54%)
  blocking collectives  55.3 us (23%)
  local copies, waits for them, and re-layouts  21.6 us (9%)
  matrix products  15.2 us (6%)
  between operations  13.5 us (6%)
  other arithmetic  4.81 us (2%)
    reduce_scatter x1, waiting for transfers between devices, on_device(): lax.psum_scatter(partial_value, 'pair', scatter_dimension=0, tiled=True)  88.9 us
    all_to_all x1, blocking collectives, on_device(): lax.all_to_all(outgoing, 'pair', split_axis=2, concat_axis=0, tiled=True)  55.3 us
    all_gather x1, waiting for transfers between devices, on_device(): lax.all_gather(received, 'integral', axis=2, tiled=True)  39.8 us
    gather x3, local copies, waits for them, and re-layouts, on_device(): chosen = jnp.take(integrals, local_tile, axis=0)  17.4 us
    dot_general x1, matrix products, on_device(): lax.dot_general(lax.all_gather(received, 'integral', axis=2, tiled=True),...  15.2 us
  transfers between devices with their start and end apart: 2, of which 2 were waited for; matrix products, arithmetic and copies ran while one was open for 8% of the time, Pallas kernels for 0%

commit v1 on v0

v1 whole, which is shorter than its diff:
```python
import functools

import jax
import jax.numpy as jnp
from jax import lax
from jax.experimental import pallas as pl
from jax.experimental.pallas import tpu as pltpu
from jax.sharding import PartitionSpec as P

MESH = pl.DeviceIdType.MESH
CORES = 2


def inner_of(count):
    return 2 ** ((count.bit_length() - 1) // 2)


def ladder_kernel(
    dims, idx_ref, t2_ref, v_ref, out_ref,
    packed, amps, ints, part, y_in, z_in,
    v_sem, own_sem, a_send, a_recv, x_send, x_recv, c_send, c_recv, y_send, y_recv, z_send, z_recv,
):
    np_, ny, ni, slots, rows, cols = dims
    nz, nx = np_ // ny, ni // CORES
    kept = t2_ref.shape[0]
    qw = v_ref.shape[2]
    p, i = lax.axis_index("pair"), lax.axis_index("integral")
    z, y = p // ny, p % ny
    x, c = i // CORES, i % CORES
    other = x * CORES + (1 - c)

    load_v = pltpu.make_async_copy(v_ref, ints, v_sem)
    load_v.start()

    barrier = pltpu.get_barrier_semaphore()
    for d in range(1, np_):
        pl.semaphore_signal(barrier, inc=1, device_id={"pair": (p + d) % np_}, device_id_type=MESH)
    for d in range(1, nx):
        pl.semaphore_signal(
            barrier, inc=1, device_id={"integral": ((x + d) % nx) * CORES + c}, device_id_type=MESH
        )
    pl.semaphore_signal(barrier, inc=1, device_id={"integral": other}, device_id_type=MESH)

    def pack(owner):
        for s in range(slots):
            at = idx_ref[owner * slots + s]
            tile = t2_ref[jnp.minimum(at, kept - 1)]
            packed[owner, s] = jnp.where(at < kept, tile, jnp.zeros_like(tile))

    def block(source, part_i):
        return amps.at[:, pl.ds(pl.multiple_of(source * rows, rows), rows), pl.ds(pl.multiple_of(part_i * cols, cols), cols)]

    def a_copy(dest, source):
        return pltpu.make_async_remote_copy(
            src_ref=packed.at[dest], dst_ref=block(source, i), send_sem=a_send.at[dest], recv_sem=a_recv.at[source],
            device_id={"pair": dest}, device_id_type=MESH,
        )

    def x_copy(source, dest_x, from_x):
        region = block(source, from_x * CORES + c)
        return pltpu.make_async_remote_copy(
            src_ref=region, dst_ref=region, send_sem=x_send.at[dest_x, source], recv_sem=x_recv.at[from_x, source],
            device_id={"integral": dest_x * CORES + c}, device_id_type=MESH,
        )

    def c_copy(source, part_x, part_c):
        region = block(source, part_x * CORES + part_c)
        return pltpu.make_async_remote_copy(
            src_ref=region, dst_ref=region, send_sem=c_send.at[part_x, source], recv_sem=c_recv.at[part_x, source],
            device_id={"integral": other}, device_id_type=MESH,
        )

    own_copy = pltpu.make_async_copy(packed.at[p], block(p, i), own_sem)

    def y_copy(zc, d):
        return pltpu.make_async_remote_copy(
            src_ref=part.at[zc, (y + d) % ny], dst_ref=y_in.at[d - 1, zc],
            send_sem=y_send.at[d - 1, zc], recv_sem=y_recv.at[d - 1, zc],
            device_id={"pair": z * ny + (y + d) % ny}, device_id_type=MESH,
        )

    def z_copy(k):
        zc = (z + nz - k) % nz
        return pltpu.make_async_remote_copy(
            src_ref=part.at[zc, y], dst_ref=z_in.at[k - 1],
            send_sem=z_send.at[k - 1], recv_sem=z_recv.at[k - 1],
            device_id={"pair": zc * ny + y}, device_id_type=MESH,
        )

    def send_order():
        for dz in range(nz):
            for dy in range(ny):
                yield dz, dy, ((z + dz) % nz) * ny + (y + dy) % ny

    first = True
    for dz, dy, dest in send_order():
        pack(dest)
        if dz == 0 and dy == 0:
            own_copy.start()
            continue
        if first:
            pl.semaphore_wait(barrier, np_ - 1 + nx - 1 + 1)
            first = False
        a_copy(dest, p).start()

    def sources(k):
        zc = (z + nz - k) % nz
        for dy in range(ny):
            yield dy, zc * ny + (y + ny - dy) % ny

    def spread(k):
        for dy, source in sources(k):
            if k == 0 and dy == 0:
                own_copy.wait()
            else:
                a_copy(p, source).wait_recv()
            for d in range(1, nx):
                x_copy(source, (x + d) % nx, x).start()
            c_copy(source, x, c).start()

    def forward(k):
        for dy, source in sources(k):
            for d in range(1, nx):
                from_x = (x + d) % nx
                x_copy(source, x, from_x).wait_recv()
                c_copy(source, from_x, c).start()

    def multiply(k):
        zc = (z + nz - k) % nz
        for dy, source in sources(k):
            for xx in range(nx):
                c_copy(source, xx, 1 - c).wait_recv()
        if k == 0:
            load_v.wait()
        span = ny * rows
        left = pl.ds(pl.multiple_of(zc * span, span), span)
        wide = 256

        @pl.loop(0, qw // wide)
        def _(n):
            right = pl.ds(pl.multiple_of(n * wide, wide), wide)
            total = jnp.zeros((span, wide), jnp.float32)
            for s in range(slots):
                total += jnp.dot(amps[s, left, :], ints[s, :, right], preferred_element_type=jnp.float32)
            part[zc, :, :, right] = total.reshape(ny, rows, wide)

        for d in range(1, ny):
            y_copy(zc, d).start()

    def reduce_y(k):
        zc = (z + nz - k) % nz
        for d in range(1, ny):
            y_copy(zc, d).wait_recv()
        total = part[zc, y]
        for d in range(1, ny):
            total += y_in[d - 1, zc]
        part[zc, y] = total
        if k > 0:
            z_copy(k).start()

    for t in range(nz + 3):
        if t < nz:
            spread(t)
        if 0 <= t - 1 < nz:
            forward(t - 1)
        if 0 <= t - 2 < nz:
            reduce_y(t - 2)
        if 0 <= t - 1 < nz:
            multiply(t - 1)

    total = part[z, y]
    for k in range(1, nz):
        z_copy(k).wait_recv()
        total += z_in[k - 1]
    out_ref[...] = (0.5 * total).astype(out_ref.dtype)

    for dz, dy, dest in send_order():
        if dz or dy:
            a_copy(dest, p).wait_send()
    for k in range(nz):
        zc = (z + nz - k) % nz
        for dy, source in sources(k):
            for d in range(1, nx):
                x_copy(source, (x + d) % nx, x).wait_send()
            for xx in range(nx):
                c_copy(source, xx, c).wait_send()
        for d in range(1, ny):
            y_copy(zc, d).wait_send()
        if k > 0:
            z_copy(k).wait_send()


def on_device(t2_tiles, keep_tile, integrals):
    np_, ni = lax.axis_size("pair"), lax.axis_size("integral")
    rows, kept, cols = t2_tiles.shape
    slots, tt, qw = integrals.shape
    ny = inner_of(np_)
    nz, nx = np_ // ny, ni // CORES
    tiles = jnp.arange(np_ * slots, dtype=jnp.int32)
    positions = jnp.arange(kept, dtype=jnp.int32)
    idx = kept + jnp.sum(jnp.where(keep_tile[None, :] == tiles[:, None], positions[None, :] - kept, 0), axis=1)
    by_tile = jnp.swapaxes(t2_tiles, 0, 1)
    dma = pltpu.SemaphoreType.DMA
    dims = (np_, ny, ni, slots, rows, cols)
    return pl.pallas_call(
        functools.partial(ladder_kernel, dims),
        out_shape=jax.ShapeDtypeStruct((rows, qw), jnp.bfloat16),
        in_specs=[
            pl.BlockSpec(memory_space=pltpu.SMEM),
            pl.BlockSpec(memory_space=pltpu.VMEM),
            pl.BlockSpec(memory_space=pl.ANY),
        ],
        out_specs=pl.BlockSpec(memory_space=pltpu.VMEM),
        scratch_shapes=[
            pltpu.VMEM((np_, slots, rows, cols), jnp.bfloat16),
            pltpu.VMEM((slots, np_ * rows, tt), jnp.bfloat16),
            pltpu.VMEM((slots, tt, qw), jnp.bfloat16),
            pltpu.VMEM((nz, ny, rows, qw), jnp.float32),
            pltpu.VMEM((ny - 1, nz, rows, qw), jnp.float32),
            pltpu.VMEM((nz - 1, rows, qw), jnp.float32),
            dma, dma,
            dma((np_,)), dma((np_,)),
            dma((nx, np_)), dma((nx, np_)),
            dma((nx, np_)), dma((nx, np_)),
            dma((ny - 1, nz)), dma((ny - 1, nz)),
            dma((nz - 1,)), dma((nz - 1,)),
        ],
        compiler_params=pltpu.CompilerParams(
            collective_id=0, has_side_effects=True, vmem_limit_bytes=60 * 1024 * 1024
        ),
    )(idx.astype(jnp.int32), by_tile, integrals)


def solution(mesh):
    placed = (P("pair", None, "integral"), P(), P("pair", None, "integral"))
    return jax.shard_map(
        on_device, mesh=mesh, in_specs=placed, out_specs=P("pair", "integral"), check_vma=False
    )
```

time: 239 us -> 129 us (0.54)
  waiting for transfers between devices: 129 us -> 0 us
  Pallas kernels: 0 us -> 125 us
  blocking collectives: 55.3 us -> 0 us
  local copies, waits for them, and re-layouts: 21.6 us -> 1.67 us
  matrix products: 15.2 us -> 0 us
  between operations: 13.5 us -> 0.01 us
  other arithmetic: 4.81 us -> 1.26 us
    pallas_call x0 -> x1, Pallas kernels: none -> 125 us  [on_device(): pl.pallas_call(functools.partial(ladder_kernel, dims), out_shape=jax.Shap...]
    reduce_scatter x1 -> x0, waiting for transfers between devices: 88.9 us -> none  [on_device(): lax.psum_scatter(partial_value, 'pair', scatter_dimension=0, tiled=True)]
    all_to_all x1 -> x0, blocking collectives: 55.3 us -> none  [on_device(): lax.all_to_all(outgoing, 'pair', split_axis=2, concat_axis=0, tiled=True)]
    all_gather x1 -> x0, waiting for transfers between devices: 39.8 us -> none  [on_device(): lax.all_gather(received, 'integral', axis=2, tiled=True)]
    gather x6 -> x0, local copies, waits for them, and re-layouts: 18.9 us -> none  [the longest x3 17.4 us: on_device(): chosen = jnp.take(integrals, local_tile, axis=0)]
    dot_general x1 -> x0, matrix products: 15.2 us -> none  [on_device(): lax.dot_general(lax.all_gather(received, 'integral', axis=2, tiled=True),...]
  transfers between devices with their start and end apart: 2 -> 0, of which waited for: 2 -> 0; matrix products, arithmetic and copies ran while one was open for 8% -> 0% of each run, Pallas kernels for 0% -> 0%
where the time goes in v1:
time: 129 us; the launch traced here: 128 us
  Pallas kernels  125 us (97%)
  local copies, waits for them, and re-layouts  1.67 us (1%)
    pallas_call x1, Pallas kernels, on_device(): pl.pallas_call(functools.partial(ladder_kernel, dims), out_shape=jax.Shap...  125 us

profile of v1, /device:TPU:0, one launch (start us, length us, event | category | flops | bytes accessed | tf_op | source)
XLA Modules:
  0.0 128.4 jit_solution(16612073124456167733)
XLA Ops:
  0.0 0.7 select_reduce_fusion
  0.7 0.5 broadcast_add_fusion.idx_ref
  1.3 125.4 %shard_map.37 = bf16[128,1024]{1,0:T(8,128)(2,1)} custom-call(s32[32]{0:T(128)} %broadcast_add_fusion.idx_ref, bf16[20,128,256]{2,1,0:T(8,128)(2,1)} %bitcast.1, bf16[4,1024,1024]{2,1,0:T(8,128)(2,1)} %v_ref.1), custom_call_target="tpu_custom_call" | custom-call | tf_op jit(solution)/shard_map/pallas_call | solution.py:205
  126.7 1.7 %copy.5 = bf16[128,1024]{1,0:T(8,128)(2,1)} copy(bf16[128,1024]{1,0:T(8,128)(2,1)} %shard_map.37) | data formatting | bytes 524288
  (1 shorter events, 0.0 us)

commit v2 on v1

v2 whole, which is shorter than its diff:
```python
import functools
import itertools

import jax
import jax.numpy as jnp
from jax import lax
from jax.experimental import pallas as pl
from jax.experimental.pallas import tpu as pltpu
from jax.sharding import PartitionSpec as P

MESH = pl.DeviceIdType.MESH
CORES = 2
HALVES = 2
CUTS = 2


def inner_of(count):
    return 2 ** ((count.bit_length() - 1) // 2)


def order_of(count, first):
    away = sorted((at for at in range(count) if at != first), key=lambda at: -abs(at - first))
    return [first] + away


def ladder_kernel(
    dims, idx_ref, t2_ref, v_ref, out_ref,
    packed, amps, ints, part, y_in, low_in, high_in,
    v_sem, own_sem, a_send, a_recv, x_send, x_recv, c_send, c_recv, y_send, y_recv, z_send, low_recv, high_recv,
):
    np_, ny, ni, slots, rows, cols = dims
    nz, nx = np_ // ny, ni // CORES
    piece = rows // CUTS
    kept = t2_ref.shape[0]
    qw = v_ref.shape[2]
    p, i = lax.axis_index("pair"), lax.axis_index("integral")
    z, y = p // ny, p % ny
    x, c = i // CORES, i % CORES
    other = x * CORES + (1 - c)
    tables = [order_of(nz, at) for at in range(nz)]
    order = [sum(jnp.where(z == at, tables[at][k], 0) for at in range(nz)) for k in range(nz)]

    load_v = pltpu.make_async_copy(v_ref, ints, v_sem)
    load_v.start()

    barrier = pltpu.get_barrier_semaphore()
    for d in range(1, np_):
        pl.semaphore_signal(barrier, inc=1, device_id={"pair": (p + d) % np_}, device_id_type=MESH)
    for d in range(1, nx):
        pl.semaphore_signal(
            barrier, inc=1, device_id={"integral": ((x + d) % nx) * CORES + c}, device_id_type=MESH
        )
    pl.semaphore_signal(barrier, inc=1, device_id={"integral": other}, device_id_type=MESH)

    def pack(owner, r):
        for s in range(slots):
            at = idx_ref[owner * slots + s]
            tile = t2_ref[jnp.minimum(at, kept - 1), r * piece : (r + 1) * piece, :]
            packed[owner, r, s] = jnp.where(at < kept, tile, jnp.zeros_like(tile))

    def block(source, r, part_i):
        start = (((source // ny) * CUTS + r) * ny + source % ny) * piece
        return amps.at[:, pl.ds(pl.multiple_of(start, piece), piece), pl.ds(pl.multiple_of(part_i * cols, cols), cols)]

    def a_copy(dest, source, r):
        return pltpu.make_async_remote_copy(
            src_ref=packed.at[dest, r], dst_ref=block(source, r, i),
            send_sem=a_send.at[dest, r], recv_sem=a_recv.at[source, r],
            device_id={"pair": dest}, device_id_type=MESH,
        )

    def x_copy(source, r, dest_x, from_x):
        region = block(source, r, from_x * CORES + c)
        return pltpu.make_async_remote_copy(
            src_ref=region, dst_ref=region, send_sem=x_send.at[dest_x, source, r], recv_sem=x_recv.at[from_x, source, r],
            device_id={"integral": dest_x * CORES + c}, device_id_type=MESH,
        )

    def c_copy(source, r, part_x, part_c):
        region = block(source, r, part_x * CORES + part_c)
        return pltpu.make_async_remote_copy(
            src_ref=region, dst_ref=region, send_sem=c_send.at[part_x, source, r], recv_sem=c_recv.at[part_x, source, r],
            device_id={"integral": other}, device_id_type=MESH,
        )

    def own_copy(r):
        return pltpu.make_async_copy(packed.at[p, r], block(p, r, i), own_sem.at[r])

    def y_copy(zc, r, d, h):
        return pltpu.make_async_remote_copy(
            src_ref=part.at[zc, r, (y + d) % ny, h], dst_ref=y_in.at[d - 1, zc, r, h],
            send_sem=y_send.at[d - 1, zc, r, h], recv_sem=y_recv.at[d - 1, zc, r, h],
            device_id={"pair": z * ny + (y + d) % ny}, device_id_type=MESH,
        )

    def up_copy(zc, r, h):
        return pltpu.make_async_remote_copy(
            src_ref=part.at[zc, r, y, h], dst_ref=low_in.at[zc, r, h],
            send_sem=z_send.at[zc, r, h], recv_sem=low_recv.at[zc, r, h],
            device_id={"pair": (p + ny) % np_}, device_id_type=MESH,
        )

    def down_copy(zc, r, h):
        return pltpu.make_async_remote_copy(
            src_ref=part.at[zc, r, y, h], dst_ref=high_in.at[zc, r, h],
            send_sem=z_send.at[zc, r, h], recv_sem=high_recv.at[zc, r, h],
            device_id={"pair": (p + np_ - ny) % np_}, device_id_type=MESH,
        )

    def send_order():
        for dz, r, dy in itertools.product(range(nz), range(CUTS), range(ny)):
            yield dz, r, dy, order[dz] * ny + (y + dy) % ny

    first = True
    for dz, r, dy, dest in send_order():
        pack(dest, r)
        if dz == 0 and dy == 0:
            own_copy(r).start()
            continue
        if first:
            pl.semaphore_wait(barrier, np_ - 1 + nx - 1 + 1)
            first = False
        a_copy(dest, p, r).start()

    def sources(k):
        zc = order[k]
        for dy in range(ny):
            yield dy, zc * ny + (y + ny - dy) % ny

    def spread(k, r):
        for dy, source in sources(k):
            if k == 0 and dy == 0:
                own_copy(r).wait()
            else:
                a_copy(p, source, r).wait_recv()
            for d in range(1, nx):
                x_copy(source, r, (x + d) % nx, x).start()
            c_copy(source, r, x, c).start()

    def forward(k, r):
        for dy, source in sources(k):
            for d in range(1, nx):
                from_x = (x + d) % nx
                x_copy(source, r, x, from_x).wait_recv()
                c_copy(source, r, from_x, c).start()

    def multiply(k, r):
        zc = order[k]
        for dy, source in sources(k):
            for xx in range(nx):
                c_copy(source, r, xx, 1 - c).wait_recv()
        if k == 0 and r == 0:
            load_v.wait()
        span = ny * piece
        left = pl.ds(pl.multiple_of((zc * CUTS + r) * span, span), span)
        wide = 256
        part_cols = qw // HALVES
        for h in range(HALVES):
            @pl.loop(0, part_cols // wide)
            def _(n):
                right = pl.ds(pl.multiple_of(h * part_cols + n * wide, wide), wide)
                into = pl.ds(pl.multiple_of(n * wide, wide), wide)
                total = jnp.zeros((span, wide), jnp.float32)
                for s in range(slots):
                    total += jnp.dot(amps[s, left, :], ints[s, :, right], preferred_element_type=jnp.float32)
                part[zc, r, :, h, :, into] = total.reshape(ny, piece, wide)

            for d in range(1, ny):
                y_copy(zc, r, d, h).start()

    def reduce_y(k, r):
        zc = order[k]
        for h in range(HALVES):
            for d in range(1, ny):
                y_copy(zc, r, d, h).wait_recv()
            total = part[zc, r, y, h]
            for d in range(1, ny):
                total += y_in[d - 1, zc, r, h]
            part[zc, r, y, h] = total
            if k > 0:
                @pl.when((z == 0) & (zc > z))
                def _():
                    up_copy(zc, r, h).start()

                @pl.when((z == nz - 1) & (zc < z))
                def _():
                    down_copy(zc, r, h).start()

    def reduce_z(k, r):
        zc = order[k]
        for h in range(HALVES):
            @pl.when((z > 0) & (zc > z))
            def _():
                up_copy(zc, r, h).wait_recv()
                part[zc, r, y, h] += low_in[zc, r, h]
                up_copy(zc, r, h).start()

            @pl.when((z < nz - 1) & (zc < z))
            def _():
                down_copy(zc, r, h).wait_recv()
                part[zc, r, y, h] += high_in[zc, r, h]
                down_copy(zc, r, h).start()

    steps = list(itertools.product(range(nz), range(CUTS)))
    for t in range(len(steps) + 3):
        if t < len(steps):
            spread(*steps[t])
        if 0 <= t - 1 < len(steps):
            forward(*steps[t - 1])
            multiply(*steps[t - 1])
        if 0 <= t - 2 < len(steps):
            reduce_y(*steps[t - 2])
        if CUTS <= t - 3 < len(steps):
            reduce_z(*steps[t - 3])

    width = qw // HALVES
    for r, h in itertools.product(range(CUTS), range(HALVES)):
        @pl.when(z > 0)
        def _():
            up_copy(z, r, h).wait_recv()
            part[z, r, y, h] += low_in[z, r, h]

        @pl.when(z < nz - 1)
        def _():
            down_copy(z, r, h).wait_recv()
            part[z, r, y, h] += high_in[z, r, h]

        out_ref[r * piece : (r + 1) * piece, h * width : (h + 1) * width] = (0.5 * part[z, r, y, h]).astype(out_ref.dtype)

    for dz, r, dy, dest in send_order():
        if dz or dy:
            a_copy(dest, p, r).wait_send()
    for k, r in steps:
        zc = order[k]
        for dy, source in sources(k):
            for d in range(1, nx):
                x_copy(source, r, (x + d) % nx, x).wait_send()
            for xx in range(nx):
                c_copy(source, r, xx, c).wait_send()
        for h in range(HALVES):
            for d in range(1, ny):
                y_copy(zc, r, d, h).wait_send()
            if k > 0:
                up_copy(zc, r, h).wait_send()


def on_device(t2_tiles, keep_tile, integrals):
    np_, ni = lax.axis_size("pair"), lax.axis_size("integral")
    rows, kept, cols = t2_tiles.shape
    slots, tt, qw = integrals.shape
    ny = inner_of(np_)
    nz, nx = np_ // ny, ni // CORES
    tiles = jnp.arange(np_ * slots, dtype=jnp.int32)
    positions = jnp.arange(kept, dtype=jnp.int32)
    idx = kept + jnp.sum(jnp.where(keep_tile[None, :] == tiles[:, None], positions[None, :] - kept, 0), axis=1)
    by_tile = jnp.swapaxes(t2_tiles, 0, 1)
    dma = pltpu.SemaphoreType.DMA
    piece = rows // CUTS
    dims = (np_, ny, ni, slots, rows, cols)
    return pl.pallas_call(
        functools.partial(ladder_kernel, dims),
        out_shape=jax.ShapeDtypeStruct((rows, qw), jnp.bfloat16),
        in_specs=[
            pl.BlockSpec(memory_space=pltpu.SMEM),
            pl.BlockSpec(memory_space=pltpu.VMEM),
            pl.BlockSpec(memory_space=pl.ANY),
        ],
        out_specs=pl.BlockSpec(memory_space=pltpu.VMEM),
        scratch_shapes=[
            pltpu.VMEM((np_, CUTS, slots, piece, cols), jnp.bfloat16),
            pltpu.VMEM((slots, np_ * rows, tt), jnp.bfloat16),
            pltpu.VMEM((slots, tt, qw), jnp.bfloat16),
            pltpu.VMEM((nz, CUTS, ny, HALVES, piece, qw // HALVES), jnp.float32),
            pltpu.VMEM((ny - 1, nz, CUTS, HALVES, piece, qw // HALVES), jnp.float32),
            pltpu.VMEM((nz, CUTS, HALVES, piece, qw // HALVES), jnp.float32),
            pltpu.VMEM((nz, CUTS, HALVES, piece, qw // HALVES), jnp.float32),
            dma, dma((CUTS,)),
            dma((np_, CUTS)), dma((np_, CUTS)),
            dma((nx, np_, CUTS)), dma((nx, np_, CUTS)),
            dma((nx, np_, CUTS)), dma((nx, np_, CUTS)),
            dma((ny - 1, nz, CUTS, HALVES)), dma((ny - 1, nz, CUTS, HALVES)),
            dma((nz, CUTS, HALVES)), dma((nz, CUTS, HALVES)), dma((nz, CUTS, HALVES)),
        ],
        compiler_params=pltpu.CompilerParams(
            collective_id=0, has_side_effects=True, vmem_limit_bytes=60 * 1024 * 1024
        ),
    )(idx.astype(jnp.int32), by_tile, integrals)


def solution(mesh):
    placed = (P("pair", None, "integral"), P(), P("pair", None, "integral"))
    return jax.shard_map(
        on_device, mesh=mesh, in_specs=placed, out_specs=P("pair", "integral"), check_vma=False
    )
```

time: 129 us -> 100 us (0.78)
  the two profiles are of different devices: /device:TPU:0 before, /device:TPU:24 now
where the time goes in v2:
time: 100 us
  Pallas kernels  97.3 us (97%)
  local copies, waits for them, and re-layouts  1.67 us (2%)
  other arithmetic  1.26 us (1%)
    pallas_call x1, Pallas kernels, on_device(): pl.pallas_call(functools.partial(ladder_kernel, dims), out_shape=jax.Shap...  97.3 us

profile of v2, /device:TPU:24, one launch (start us, length us, event | category | flops | bytes accessed | tf_op | source)
XLA Modules:
  0.0 100.2 jit_solution(12837891291284288688)
XLA Ops:
  0.0 0.7 select_reduce_fusion
  0.7 0.5 broadcast_add_fusion.idx_ref
  1.3 97.3 %shard_map.37 = bf16[128,1024]{1,0:T(8,128)(2,1)} custom-call(s32[32]{0:T(128)} %broadcast_add_fusion.idx_ref, bf16[20,128,256]{2,1,0:T(8,128)(2,1)} %bitcast.1, bf16[4,1024,1024]{2,1,0:T(8,128)(2,1)} %v_ref.1), custom_call_target="tpu_custom_call" | custom-call | tf_op jit(solution)/shard_map/pallas_call | solution.py:260
  98.5 1.7 %copy.5 = bf16[128,1024]{1,0:T(8,128)(2,1)} copy(bf16[128,1024]{1,0:T(8,128)(2,1)} %shard_map.37) | data formatting | bytes 524288
  (1 shorter events, 0.0 us)
